TPU v7x, 256 devices: a whole 4x4x8 slice. The times are simulated.
256 devices in a mesh: gen: 8 (over z_lo, core), user: 16 (over x, y), cand: 2 (over z_hi).
Axes of the slice: x: 4, y: 4, z: 8 (z_hi: 2, z_lo: 4; z = z_hi * 4 + z_lo), core: 2. Of those that a mesh axis runs over, the one named last changes fastest.
Arguments:
- states: bfloat16 [16384, 4096], P(('user', 'cand')), may hold values from -6 to 6
- norm_gain: float32 [4096], replicated, may hold values from 0.1 to 1.9
- gate_weight: bfloat16 [4096, 7168], P('user', 'gen'), may hold values from -0.09375 to 0.09375
- up_weight: bfloat16 [4096, 7168], P('user', 'gen'), may hold values from -0.09375 to 0.09375
- down_weight: bfloat16 [7168, 4096], P('gen', 'user'), may hold values from -0.0625 to 0.0625
- proj_weight: bfloat16 [4096, 1024], P('gen'), may hold values from -0.09375 to 0.09375
- private_rows: bfloat16 [32768, 1024], P(('gen', 'user')), may hold values from -6 to 6
- enc_weight: bfloat16 [1024, 1024], replicated, may hold values from -0.1875 to 0.1875
- user_ids: int32 [32768], P(('gen', 'user')), may hold values from 0 to 31
Outputs:
- votes: float32 [16, 2, 128], P(None, 'cand')
Inputs may be any that keep to these rules, and one draw needn't show every extreme that they name: `user_ids`: a user is a pair of a block of 256 rows and a slot; no user has rows in two blocks.
All inputs are finite; a program needn't handle non-finite values.
Results may differ from a plain program's by a relative error of at most 0.0025.
Values may be sent and summed in bfloat16 or wider, within the bound.
No kernel may reach another device: no remote copies, remote signals or barrier semaphores. Data moves between devices by JAX's collectives and lax.ppermute only.
A program may use at most 128 MiB of HBM per device.

v0:
```python
import jax
import jax.numpy as jnp
from jax import lax
from jax.sharding import PartitionSpec as P

STEPS = 4
CAP = 8
USERS_DEV = 32


def unit_rows(matrix):
    return (matrix * lax.rsqrt(jnp.sum(matrix * matrix, axis=1, keepdims=True) + 1e-06)).astype(
        jnp.bfloat16
    )


def project_in(inputs, gate_part, up_part):

    def add_rows(piece):
        return jnp.dot(inputs, piece, preferred_element_type=jnp.float32)

    gate = add_rows(lax.all_gather(gate_part, "user", axis=0, tiled=True))
    up_proj = add_rows(lax.all_gather(up_part, "user", axis=0, tiled=True))
    return (gate, up_proj)


def shards(
    states,
    norm_gain,
    gate_weight,
    up_weight,
    down_weight,
    proj_weight,
    private_rows,
    enc_weight,
    user_ids,
):
    tok_rows, width_model = states.shape
    groups = tok_rows // STEPS
    values = states.astype(jnp.float32)
    normed = (
        values * lax.rsqrt(jnp.mean(values * values, axis=1, keepdims=True) + 1e-05) * norm_gain
    ).astype(jnp.bfloat16)
    gate_part, up_part, down_part = (gate_weight, up_weight, down_weight)
    gate, up_proj = project_in(normed, gate_part, up_part)
    hidden = (jax.nn.silu(gate) * up_proj).astype(jnp.bfloat16)
    mixed = jnp.dot(
        hidden,
        lax.all_gather(down_part, "user", axis=1, tiled=True),
        preferred_element_type=jnp.float32,
    )
    pooled_mlp = jnp.sum(mixed.reshape(-1, STEPS, width_model), axis=1)
    pooled_mlp = lax.psum_scatter(pooled_mlp, "gen", scatter_dimension=1, tiled=True)
    slab_width = pooled_mlp.shape[1]
    own_cols = lax.dynamic_slice_in_dim(values, lax.axis_index("gen") * slab_width, slab_width, 1)
    pooled_in = jnp.sum(own_cols.reshape(groups, STEPS, slab_width), axis=1)
    pooled = ((pooled_in + pooled_mlp) / STEPS).astype(jnp.bfloat16)
    partial_emb = jnp.dot(pooled, proj_weight, preferred_element_type=jnp.float32)
    embedding = lax.psum(partial_emb, "gen")
    candidate = unit_rows(embedding)
    every_cand = lax.all_gather(candidate, "user", axis=0, tiled=True)
    encoded = unit_rows(jnp.dot(private_rows, enc_weight, preferred_element_type=jnp.float32))
    scores = lax.dot_general(
        encoded, every_cand, (((1,), (1,)), ((), ())), preferred_element_type=jnp.float32
    )
    kernel = jnp.exp(scores * 60.0)
    totals = lax.psum(jnp.sum(kernel, axis=1), "cand")
    member = (user_ids[:, None] == jnp.arange(USERS_DEV, dtype=jnp.int32)[None, :]).astype(
        jnp.float32
    )
    counts = jnp.sum(member, axis=0)
    limit = jnp.minimum(1.0, CAP / jnp.maximum(counts, 1.0))
    row_cap = jnp.dot(member, limit, precision=lax.Precision.HIGHEST)
    row_total = private_rows.shape[0] * lax.axis_size("gen") * lax.axis_size("user")
    cand_total = every_cand.shape[0] * lax.axis_size("cand")
    weight_rows = row_cap / totals * (cand_total / row_total)
    partial_votes = jnp.dot(weight_rows, kernel, precision=lax.Precision.HIGHEST)
    votes = lax.psum(partial_votes, ("gen", "user"))
    return votes.reshape(lax.axis_size("user"), 1, groups)


def solution(mesh):
    return jax.shard_map(
        shards,
        mesh=mesh,
        in_specs=(
            P(("user", "cand"), None),
            P(),
            P("user", "gen"),
            P("user", "gen"),
            P("gen", "user"),
            P("gen", None),
            P(("gen", "user"), None),
            P(),
            P(("gen", "user")),
        ),
        out_specs=P(None, "cand", None),
        check_vma=False,
    )
```

profile of v0, /device:TPU:0, one launch (start us, length us, event | category | flops | bytes accessed | tf_op | source)
XLA Modules:
  0.0 810.1 jit_solution(10870717847516051505)
XLA Ops:
  6.5 0.7 all-gather.5.cloned.1.call-update
  7.3 0.0 all-gather.7.cloned.1.call-start
  7.3 0.7 all-gather.7.cloned.1.call-update
  8.1 0.7 all-gather.9.cloned.1.call-update
  8.7 0.0 reduce-scatter.2.cloned.1.call-start
  8.8 3.1 multiply_reduce_fusion
  11.9 70.3 %all-gather.5.cloned.1.call-done = bf16[4096,896]{1,0:T(8,128)(2,1)} async-done(((bf16[256,896]{1,0:T(8,128)(2,1)}), bf16[4096,896]{1,0:T(8,128)(2,1)}) %all-gather.5.cloned.1.call-update) | async-done | bytes 7340048 | tf_op jit(solution)/shard_map/all_gather | solution.py:22
  82.2 10.1 %fusion.1 = f32[512,896]{1,0:T(8,128)} fusion(bf16[4096,896]{1,0:T(8,128)(2,1)} %all-gather.5.cloned.1.call-done, f32[4096]{0:T(1024)S(1)} %copy-done.1, f32[512]{0:T(512)S(1)} %add_rsqrt_fusion, bf16[512,4096]{1,0:T(8,128)(2,1)} %param.9), kind=kOutput, calls=%fused_computation.5 | convolution fusion | flops 3766484992 | bytes 13387776 | tf_op jit(solution)/shard_map/dot_general | solution.py:20
  92.3 63.2 %all-gather.7.cloned.1.call-done = bf16[4096,896]{1,0:T(8,128)(2,1)} async-done(((bf16[256,896]{1,0:T(8,128)(2,1)}), bf16[4096,896]{1,0:T(8,128)(2,1)}) %all-gather.7.cloned.1.call-update) | async-done | bytes 7340048 | tf_op jit(solution)/shard_map/all_gather | solution.py:23
  155.6 79.3 %all-gather.9.cloned.1.call-done = bf16[896,4096]{1,0:T(8,128)(2,1)} async-done(((bf16[896,256]{1,0:T(8,128)(2,1)}), bf16[896,4096]{1,0:T(8,128)(2,1)}) %all-gather.9.cloned.1.call-update) | async-done | bytes 7340048 | tf_op jit(solution)/shard_map/all_gather | solution.py:49
  234.8 17.4 %fusion.2 = f32[512,4096]{1,0:T(8,128)} fusion(bf16[896,4096]{1,0:T(8,128)(2,1)} %all-gather.9.cloned.1.call-done, f32[512,896]{1,0:T(8,128)} %fusion.1, bf16[4096,896]{1,0:T(8,128)(2,1)} %all-gather.7.cloned.1.call-done, f32[4096]{0:T(1024)S(1)} %copy-done.1, f32[512]{0:T(512)S(1)} %add_rsqrt_fusion, bf16[512,4096]{1,0:T(8,128)(2,1)} %param.9), kind=kOutput, calls=%fused_computation.9 | convolution fusion | flops 7527333888 | bytes 29116416 | tf_op jit(solution)/shard_map/dot_general | solution.py:47
  252.2 9.8 %reshape.32 = f32[128,4,4096]{2,1,0:T(4,128)} reshape(f32[512,4096]{1,0:T(8,128)} %fusion.2) | data formatting | bytes 16777216 | tf_op jit(solution)/shard_map/reshape | solution.py:52
  262.0 10.0 %reduce_sum.67 = f32[128,4096]{1,0:T(8,128)} reduce(f32[128,4,4096]{2,1,0:T(4,128)} %reshape.32, f32[]{:T(128)} %constant.15.clone.1), dimensions={1}, to_apply=%region_4.5 | reduce | flops 1572864 | bytes 10485764 | tf_op jit(solution)/shard_map/reduce_sum | solution.py:52
  272.1 0.0 all-reduce.2.cloned.1.call-start
  272.1 6.5 convert_element_type.23
  278.6 1.3 constant_dynamic-slice_fusion
  279.9 1.3 reshape.31
  281.2 1.8 reduce_sum.65
  283.1 29.9 %reduce-scatter.2.cloned.1.call-done = f32[128,512]{1,0:T(8,128)} async-done(((f32[128,4096]{1,0:T(8,128)}), f32[128,512]{1,0:T(8,128)}) %reduce-scatter.2.cloned.1.call-update) | async-done | bytes 262160 | tf_op jit(solution)/shard_map/reduce_scatter | solution.py:53
  313.0 2.4 fusion.4
  315.4 0.3 all-gather.11.cloned.1.call-start
  315.7 70.7 %all-reduce.2.cloned.1.call-done = f32[128,1024]{1,0:T(8,128)} async-done(((f32[128,1024]{1,0:T(8,128)}), f32[128,1024]{1,0:T(8,128)}) %all-reduce.2.cloned.1.call-update) | async-done | bytes 524304 | tf_op jit(solution)/shard_map/psum | solution.py:59
  386.3 1.2 multiply_reduce_fusion.2
  387.5 1.8 multiply_convert_fusion.8
  389.4 0.1 convert_reduce_fusion
  389.5 1.8 multiply_reduce_fusion.1
  391.3 0.1 fusion.6
  391.5 53.5 %all-gather.11.cloned.1.call-done = bf16[2048,1024]{1,0:T(8,128)(2,1)} async-done(((bf16[128,1024]{1,0:T(8,128)(2,1)}), bf16[2048,1024]{1,0:T(8,128)(2,1)}) %all-gather.11.cloned.1.call-update) | async-done | bytes 4194320 | tf_op jit(solution)/shard_map/all_gather | solution.py:61
  445.0 4.9 fusion.16
  449.8 8.8 %psum.22 = f32[256]{0:T(256)S(1)} all-reduce(f32[256]{0:T(256)S(1)} %get-tuple-element.7), channel_id=1, replica_groups=mesh['gen'=8,'user'=16,'cand'=2] {'cand'}, use_global_device_ids=true, to_apply=%region_9.10 | all-reduce | flops 256 | bytes 2048 | tf_op jit(solution)/shard_map/psum | solution.py:67
  458.6 2.7 convolution_bitcast_fusion
  461.3 341.9 %psum.23 = f32[16,1,128]{2,1,0:T(1,128)} all-reduce(f32[16,1,128]{2,1,0:T(1,128)S(1)} %convolution_bitcast_fusion), channel_id=1, replica_groups=mesh['gen'=8,'user'=16,'cand'=2] {'gen','user'}, use_global_device_ids=true, to_apply=%region_10.11 | all-reduce | flops 2048 | bytes 16384 | tf_op jit(solution)/shard_map/psum | solution.py:78
  (15 shorter events, 0.1 us)
Async XLA Ops:
  6.5 383.0 %copy-start = (bf16[1024,1024]{1,0:T(8,128)(2,1)S(1)}, bf16[1024,1024]{1,0:T(8,128)(2,1)}, u32[]{:S(2)}) copy-start(bf16[1024,1024]{1,0:T(8,128)(2,1)} %param.16) | copy-start | bytes 6291460
  6.5 75.7 %copy-start.1 = (f32[4096]{0:T(1024)S(1)}, f32[4096]{0:T(1024)}, u32[]{:S(2)}) copy-start(f32[4096]{0:T(1024)} %param.10) | copy-start | bytes 49156
  6.5 75.7 %all-gather.5.cloned.1.call-start = ((), (), s32[]{:S(2)}) async-start(), calls=%async_computation.1 | async-start | bytes 7798784 | tf_op jit(solution)/shard_map/all_gather | solution.py:22
  7.3 148.3 %all-gather.7.cloned.1.call-start = ((), (), s32[]{:S(2)}) async-start(), calls=%async_computation.2 | async-start | bytes 7798784 | tf_op jit(solution)/shard_map/all_gather | solution.py:23
  8.0 226.8 %all-gather.9.cloned.1.call-start = ((), (), s32[]{:S(2)}) async-start(), calls=%async_computation.3 | async-start | bytes 7798784 | tf_op jit(solution)/shard_map/all_gather | solution.py:49
  8.7 304.2 %reduce-scatter.2.cloned.1.call-start = ((), (), s32[]{:S(2)}) async-start(), calls=%async_computation.4 | async-start | bytes 2359296 | tf_op jit(solution)/shard_map/reduce_scatter | solution.py:53
  272.1 114.3 %all-reduce.2.cloned.1.call-start = ((), (), s32[]{:S(2)}) async-start(), calls=%async_computation.5 | async-start | bytes 1048576 | tf_op jit(solution)/shard_map/psum | solution.py:59
  279.9 109.5 %copy-start.2 = (s32[256]{0:T(256)S(1)}, s32[256]{0:T(256)}, u32[]{:S(2)}) copy-start(s32[256]{0:T(256)} %param.17) | copy-start | bytes 3076
  315.4 129.5 %all-gather.11.cloned.1.call-start = ((), (), s32[]{:S(2)}) async-start(), calls=%async_computation.6 | async-start | bytes 4456448 | tf_op jit(solution)/shard_map/all_gather | solution.py:61
Sparse Core Ops, SparseCore 0:
  9.8 72.3 all-gather.4
  84.7 70.8 all-gather.6
  158.0 76.7 all-gather.8
  272.2 40.7 reduce-scatter.1
  315.5 70.7 all-reduce.1
  389.5 55.4 all-gather.10
where the time goes:
time: 811 us; the launch traced here: 810 us
  waiting for transfers between devices  369 us (45%)
  blocking collectives  351 us (43%)
  matrix products  39.5 us (5%)
  other arithmetic  24.6 us (3%)
  between operations  13.5 us (2%)
  local copies, waits for them, and re-layouts  12.4 us (2%)
    psum x1, blocking collectives, shards(): votes = lax.psum(partial_votes, ('gen', 'user'))  342 us
    all_gather x1, waiting for transfers between devices, shards(): lax.all_gather(down_part, 'user', axis=1, tiled=True)  79.3 us
    psum x1, waiting for transfers between devices, shards(): embedding = lax.psum(partial_emb, 'gen')  70.7 us
    all_gather x1, waiting for transfers between devices, project_in(): gate = add_rows(lax.all_gather(gate_part, 'user', axis=0, tiled=True))  70.3 us
    all_gather x1, waiting for transfers between devices, project_in(): up_proj = add_rows(lax.all_gather(up_part, 'user', axis=0, tiled=True))  63.2 us
    all_gather x1, waiting for transfers between devices, shards(): every_cand = lax.all_gather(candidate, 'user', axis=0, tiled=True)  53.5 us
    reduce_scatter x1, waiting for transfers between devices, shards(): lax.psum_scatter(pooled_mlp, 'gen', scatter_dimension=1, tiled=True)  29.9 us
    dot_general x1, matrix products, shards(): jnp.dot(hidden, lax.all_gather(down_part, 'user', axis=1, tiled=True), pr...  17.4 us
  transfers between devices with their start and end apart: 6, of which 6 were waited for; matrix products, arithmetic and copies ran while one was open for 3% of the time, Pallas kernels for 0%

commit v1 on v0

--- a/solution.py
+++ b/solution.py
@@ -6,6 +6,19 @@
 STEPS = 4
 CAP = 8
 USERS_DEV = 32
+
+
+def gather_around(x, axis, dim):
+    ways = lax.axis_size(axis)
+    up = [(d, (d + 1) % ways) for d in range(ways)]
+    down = [(d, (d - 1) % ways) for d in range(ways)]
+    earlier, later = ([x], [x])
+    for _ in range(ways // 2):
+        earlier.append(lax.ppermute(earlier[-1], axis, up))
+    for _ in range((ways - 1) // 2):
+        later.append(lax.ppermute(later[-1], axis, down))
+    line = jnp.concatenate([*earlier[::-1], *later[1:]], axis=dim)
+    return jnp.roll(line, (lax.axis_index(axis) - ways // 2) * x.shape[dim], axis=dim)
 
 
 def unit_rows(matrix):
@@ -44,11 +57,7 @@
     gate_part, up_part, down_part = (gate_weight, up_weight, down_weight)
     gate, up_proj = project_in(normed, gate_part, up_part)
     hidden = (jax.nn.silu(gate) * up_proj).astype(jnp.bfloat16)
-    mixed = jnp.dot(
-        hidden,
-        lax.all_gather(down_part, "user", axis=1, tiled=True),
-        preferred_element_type=jnp.float32,
-    )
+    mixed = jnp.dot(hidden, gather_around(down_part, "user", 1), preferred_element_type=jnp.float32)
     pooled_mlp = jnp.sum(mixed.reshape(-1, STEPS, width_model), axis=1)
     pooled_mlp = lax.psum_scatter(pooled_mlp, "gen", scatter_dimension=1, tiled=True)
     slab_width = pooled_mlp.shape[1]

time: 811 us -> 785 us (0.968)
  waiting for transfers between devices: 369 us -> 262 us
  local copies, waits for them, and re-layouts: 12.4 us -> 54.5 us
  starting transfers between devices: 0.42 us -> 38.4 us
    ppermute x0 -> x15, waiting for transfers between devices: none -> 112 us  [the longest x8 112 us: gather_around(): earlier.append(lax.ppermute(earlier[-1], axis, up))]
    all_gather x1 -> x0, waiting for transfers between devices: 79.3 us -> none  [shards(): lax.all_gather(down_part, 'user', axis=1, tiled=True)]
    all_gather x1, waiting for transfers between devices: 70.3 us -> 0.01 us  [project_in(): gate = add_rows(lax.all_gather(gate_part, 'user', axis=0, tiled=True))]
    all_gather x1, waiting for transfers between devices: 63.2 us -> 0.01 us  [project_in(): up_proj = add_rows(lax.all_gather(up_part, 'user', axis=0, tiled=True))]
    unnamed x6 -> x63, local copies, waits for them, and re-layouts: 0.01 us -> 41.3 us
    ppermute x0 -> x15, starting transfers between devices: none -> 37.9 us  [the longest x7 37.8 us: gather_around(): later.append(lax.ppermute(later[-1], axis, down))]
  transfers between devices with their start and end apart: 6 -> 20, of which waited for: 6 -> 11; matrix products, arithmetic and copies ran while one was open for 3% -> 9% of each run, Pallas kernels for 0% -> 0%
where the time goes in v1:
time: 785 us; the launch traced here: 783 us
  blocking collectives  351 us (45%)
  waiting for transfers between devices  262 us (33%)
  local copies, waits for them, and re-layouts  54.5 us (7%)
  matrix products  39.5 us (5%)
  starting transfers between devices  38.4 us (5%)
  other arithmetic  24.6 us (3%)
  between operations  13.3 us (2%)
    psum x1, blocking collectives, shards(): votes = lax.psum(partial_votes, ('gen', 'user'))  342 us
    ppermute x8, waiting for transfers between devices, gather_around(): earlier.append(lax.ppermute(earlier[-1], axis, up))  112 us
    psum x1, waiting for transfers between devices, shards(): embedding = lax.psum(partial_emb, 'gen')  70.7 us
    all_gather x1, waiting for transfers between devices, shards(): every_cand = lax.all_gather(candidate, 'user', axis=0, tiled=True)  53.5 us
    unnamed x63, local copies, waits for them, and re-layouts  41.3 us
    ppermute x7, starting transfers between devices, gather_around(): later.append(lax.ppermute(later[-1], axis, down))  37.8 us
    reduce_scatter x1, waiting for transfers between devices, shards(): lax.psum_scatter(pooled_mlp, 'gen', scatter_dimension=1, tiled=True)  24.8 us
    dot_general x1, matrix products, shards(): jnp.dot(hidden, gather_around(down_part, 'user', 1), preferred_element_ty...  17.4 us
  transfers between devices with their start and end apart: 20, of which 11 were waited for; matrix products, arithmetic and copies ran while one was open for 9% of the time, Pallas kernels for 0%

profile of v1, /device:TPU:0, one launch (start us, length us, event | category | flops | bytes accessed | tf_op | source)
XLA Modules:
  0.0 783.3 jit_solution(1010670928891532978)
XLA Ops:
  8.1 14.2 %collective-permute-done = bf16[896,256]{1,0:T(8,128)(2,1)S(1)} collective-permute-done((bf16[896,256]{1,0:T(8,128)(2,1)}, bf16[896,256]{1,0:T(8,128)(2,1)S(1)}, u32[]{:S(2)}, u32[]{:S(2)}) %collective-permute-start) | collective-permute-done | bytes 458784 | tf_op jit(solution)/shard_map/ppermute | solution.py:17
  22.4 5.3 collective-permute-start.8
  27.7 16.3 %collective-permute-done.1 = bf16[896,256]{1,0:T(8,128)(2,1)S(1)} collective-permute-done((bf16[896,256]{1,0:T(8,128)(2,1)S(1)}, bf16[896,256]{1,0:T(8,128)(2,1)S(1)}, u32[]{:S(2)}, u32[]{:S(2)}) %collective-permute-start.1) | collective-permute-done | bytes 458784 | tf_op jit(solution)/shard_map/ppermute | solution.py:17
  44.0 5.3 collective-permute-start.9
  49.4 8.7 %collective-permute-done.2 = bf16[896,256]{1,0:T(8,128)(2,1)S(1)} collective-permute-done((bf16[896,256]{1,0:T(8,128)(2,1)S(1)}, bf16[896,256]{1,0:T(8,128)(2,1)S(1)}, u32[]{:S(2)}, u32[]{:S(2)}) %collective-permute-start.2) | collective-permute-done | bytes 458784 | tf_op jit(solution)/shard_map/ppermute | solution.py:17
  58.1 5.4 collective-permute-start.10
  63.5 20.8 %collective-permute-done.3 = bf16[896,256]{1,0:T(8,128)(2,1)S(1)} collective-permute-done((bf16[896,256]{1,0:T(8,128)(2,1)S(1)}, bf16[896,256]{1,0:T(8,128)(2,1)S(1)}, u32[]{:S(2)}, u32[]{:S(2)}) %collective-permute-start.3) | collective-permute-done | bytes 458784 | tf_op jit(solution)/shard_map/ppermute | solution.py:17
  84.3 5.4 collective-permute-start.11
  89.7 21.0 %collective-permute-done.4 = bf16[896,256]{1,0:T(8,128)(2,1)S(1)} collective-permute-done((bf16[896,256]{1,0:T(8,128)(2,1)S(1)}, bf16[896,256]{1,0:T(8,128)(2,1)S(1)}, u32[]{:S(2)}, u32[]{:S(2)}) %collective-permute-start.4) | collective-permute-done | bytes 458784 | tf_op jit(solution)/shard_map/ppermute | solution.py:17
  110.7 5.3 collective-permute-start.12
  116.0 10.8 %collective-permute-done.5 = bf16[896,256]{1,0:T(8,128)(2,1)} collective-permute-done((bf16[896,256]{1,0:T(8,128)(2,1)S(1)}, bf16[896,256]{1,0:T(8,128)(2,1)}, u32[]{:S(2)}, u32[]{:S(2)}) %collective-permute-start.5) | collective-permute-done | bytes 458784 | tf_op jit(solution)/shard_map/ppermute | solution.py:17
  126.9 5.4 collective-permute-start.13
  132.3 16.8 %collective-permute-done.6 = bf16[896,256]{1,0:T(8,128)(2,1)} collective-permute-done((bf16[896,256]{1,0:T(8,128)(2,1)}, bf16[896,256]{1,0:T(8,128)(2,1)}, u32[]{:S(2)}, u32[]{:S(2)}) %collective-permute-start.6) | collective-permute-done | bytes 458784 | tf_op jit(solution)/shard_map/ppermute | solution.py:17
  149.1 3.1 multiply_reduce_fusion
  152.2 5.6 collective-permute-start.14
  157.8 3.3 collective-permute-done.7
  165.7 1.9 constant_dynamic-update-slice_fusion.28
  167.6 1.9 constant_dynamic-update-slice_fusion.27
  169.6 1.9 constant_dynamic-update-slice_fusion.26
  203.2 10.1 %fusion.3 = f32[512,896]{1,0:T(8,128)} fusion(bf16[4096,896]{1,0:T(8,128)(2,1)} %all-gather.4.cloned.1.call-done, f32[4096]{0:T(1024)S(1)} %copy-done.14, f32[512]{0:T(512)S(1)} %add_rsqrt_fusion, bf16[512,4096]{1,0:T(8,128)(2,1)} %param.9), kind=kOutput, calls=%fused_computation.7 | convolution fusion | flops 3766484992 | bytes 13387776 | tf_op jit(solution)/shard_map/dot_general | solution.py:33
  213.3 17.4 %fusion = f32[512,4096]{1,0:T(8,128)} fusion(bf16[896,8192]{1,0:T(8,128)(2,1)} %constant_dynamic-update-slice_fusion, s32[]{:T(128)S(6)} %select_n.18, f32[512,896]{1,0:T(8,128)} %fusion.3, bf16[4096,896]{1,0:T(8,128)(2,1)} %all-gather.6.cloned.1.call-done, f32[4096]{0:T(1024)S(1)} %copy-done.14, f32[512]{0:T(512)S(1)} %add_rsqrt_fusion, ...), kind=kOutput, calls=%fused_computation.2 | convolution fusion | flops 7527333888 | bytes 29116420 | tf_op jit(solution)/shard_map/dot_general | solution.py:60
  230.7 9.8 %reshape.32 = f32[128,4,4096]{2,1,0:T(4,128)} reshape(f32[512,4096]{1,0:T(8,128)} %fusion) | data formatting | bytes 16777216 | tf_op jit(solution)/shard_map/reshape | solution.py:61
  240.5 10.1 %reduce_sum.67 = f32[128,4096]{1,0:T(8,128)} reduce(f32[128,4,4096]{2,1,0:T(4,128)} %reshape.32, f32[]{:T(128)} %constant.23.clone.1), dimensions={1}, to_apply=%region_4.5 | reduce | flops 1572864 | bytes 10485764 | tf_op jit(solution)/shard_map/reduce_sum | solution.py:61
  250.7 6.5 convert_element_type.23
  261.6 24.8 %reduce-scatter.2.cloned.1.call-done = f32[128,512]{1,0:T(8,128)} async-done(((f32[128,4096]{1,0:T(8,128)}), f32[128,512]{1,0:T(8,128)}) %reduce-scatter.2.cloned.1.call-update) | async-done | bytes 262160 | tf_op jit(solution)/shard_map/reduce_scatter | solution.py:62
  286.4 2.4 fusion.5
  289.2 70.7 %all-reduce.2.cloned.1.call-done = f32[128,1024]{1,0:T(8,128)} async-done(((f32[128,1024]{1,0:T(8,128)}), f32[128,1024]{1,0:T(8,128)}) %all-reduce.2.cloned.1.call-update) | async-done | bytes 524304 | tf_op jit(solution)/shard_map/psum | solution.py:68
  365.0 53.5 %all-gather.8.cloned.1.call-done = bf16[2048,1024]{1,0:T(8,128)(2,1)} async-done(((bf16[128,1024]{1,0:T(8,128)(2,1)}), bf16[2048,1024]{1,0:T(8,128)(2,1)}) %all-gather.8.cloned.1.call-update) | async-done | bytes 4194320 | tf_op jit(solution)/shard_map/all_gather | solution.py:70
  418.5 4.9 fusion.18
  423.3 8.8 %psum.22 = f32[256]{0:T(256)S(1)} all-reduce(f32[256]{0:T(256)S(1)} %get-tuple-element.7), channel_id=1, replica_groups=mesh['gen'=8,'user'=16,'cand'=2] {'cand'}, use_global_device_ids=true, to_apply=%region_9.10 | all-reduce | flops 256 | bytes 2048 | tf_op jit(solution)/shard_map/psum | solution.py:76
  432.2 2.7 convolution_bitcast_fusion
  434.8 341.9 %psum.23 = f32[16,1,128]{2,1,0:T(1,128)} all-reduce(f32[16,1,128]{2,1,0:T(1,128)S(1)} %convolution_bitcast_fusion), channel_id=1, replica_groups=mesh['gen'=8,'user'=16,'cand'=2] {'gen','user'}, use_global_device_ids=true, to_apply=%region_10.11 | all-reduce | flops 2048 | bytes 16384 | tf_op jit(solution)/shard_map/psum | solution.py:87
  (100 shorter events, 48.0 us)
Async XLA Ops:
  6.5 356.5 %copy-start = (bf16[1024,1024]{1,0:T(8,128)(2,1)S(1)}, bf16[1024,1024]{1,0:T(8,128)(2,1)}, u32[]{:S(2)}) copy-start(bf16[1024,1024]{1,0:T(8,128)(2,1)} %param.16) | copy-start | bytes 6291460
  6.5 188.0 %copy-start.1 = (bf16[896,256]{1,0:T(8,128)(2,1)S(1)}, bf16[896,256]{1,0:T(8,128)(2,1)}, u32[]{:S(2)}) copy-start(bf16[896,256]{1,0:T(8,128)(2,1)} %param.13) | copy-start | bytes 1376260
  6.5 196.7 %all-gather.4.cloned.1.call-start = ((), (), s32[]{:S(2)}) async-start(), calls=%async_computation.1 | async-start | bytes 7798784 | tf_op jit(solution)/shard_map/all_gather | solution.py:35
  7.3 206.0 %all-gather.6.cloned.1.call-start = ((), (), s32[]{:S(2)}) async-start(), calls=%async_computation.2 | async-start | bytes 7798784 | tf_op jit(solution)/shard_map/all_gather | solution.py:36
  8.0 278.4 %reduce-scatter.2.cloned.1.call-start = ((), (), s32[]{:S(2)}) async-start(), calls=%async_computation.3 | async-start | bytes 2359296 | tf_op jit(solution)/shard_map/reduce_scatter | solution.py:62
  8.1 14.3 %collective-permute-start = (bf16[896,256]{1,0:T(8,128)(2,1)}, bf16[896,256]{1,0:T(8,128)(2,1)S(1)}, u32[]{:S(2)}, u32[]{:S(2)}) collective-permute-start(bf16[896,256]{1,0:T(8,128)(2,1)} %param.13), channel_id=1, source_target_pairs={{0,2},{2,4},{4,6},{6,8},{8,10},{10,12},{12,14},{14,16},{16,18},{18... | collective-permute-start | bytes 1376264 | tf_op jit(solution)/shard_map/ppermute | solution.py:17
  22.4 21.7 %collective-permute-start.1 = (bf16[896,256]{1,0:T(8,128)(2,1)S(1)}, bf16[896,256]{1,0:T(8,128)(2,1)S(1)}, u32[]{:S(2)}, u32[]{:S(2)}) collective-permute-start(bf16[896,256]{1,0:T(8,128)(2,1)S(1)} %collective-permute-done), channel_id=1, source_target_pairs={{0,2},{2,4},{4,6},{6,8},{8,10},{10,12},{12,14},{14,16},{16,18},{18... | collective-permute-start | bytes 1376264 | tf_op jit(solution)/shard_map/ppermute | solution.py:17
  22.4 21.7 %collective-permute-start.8 = (bf16[896,256]{1,0:T(8,128)(2,1)}, bf16[896,256]{1,0:T(8,128)(2,1)S(1)}, u32[]{:S(2)}, u32[]{:S(2)}) collective-permute-start(bf16[896,256]{1,0:T(8,128)(2,1)} %param.13), channel_id=1, source_target_pairs={{0,30},{2,0},{4,2},{6,4},{8,6},{10,8},{12,10},{14,12},{16,14},{18,... | collective-permute-start | bytes 1376264 | tf_op jit(solution)/shard_map/ppermute | solution.py:19
  44.0 14.1 %collective-permute-start.2 = (bf16[896,256]{1,0:T(8,128)(2,1)S(1)}, bf16[896,256]{1,0:T(8,128)(2,1)S(1)}, u32[]{:S(2)}, u32[]{:S(2)}) collective-permute-start(bf16[896,256]{1,0:T(8,128)(2,1)S(1)} %collective-permute-done.1), channel_id=1, source_target_pairs={{0,2},{2,4},{4,6},{6,8},{8,10},{10,12},{12,14},{14,16},{16,18},{18... | collective-permute-start | bytes 1376264 | tf_op jit(solution)/shard_map/ppermute | solution.py:17
  44.0 14.1 %collective-permute-start.9 = (bf16[896,256]{1,0:T(8,128)(2,1)S(1)}, bf16[896,256]{1,0:T(8,128)(2,1)S(1)}, u32[]{:S(2)}, u32[]{:S(2)}) collective-permute-start(bf16[896,256]{1,0:T(8,128)(2,1)S(1)} %collective-permute-done.8), channel_id=1, source_target_pairs={{0,30},{2,0},{4,2},{6,4},{8,6},{10,8},{12,10},{14,12},{16,14},{18,... | collective-permute-start | bytes 1376264 | tf_op jit(solution)/shard_map/ppermute | solution.py:19
  58.1 26.2 %copy-start.6 = (bf16[896,256]{1,0:T(8,128)(2,1)}, bf16[896,256]{1,0:T(8,128)(2,1)S(1)}, u32[]{:S(2)}) copy-start(bf16[896,256]{1,0:T(8,128)(2,1)S(1)} %collective-permute-done.2) | copy-start | bytes 1376260
  58.1 26.2 %collective-permute-start.3 = (bf16[896,256]{1,0:T(8,128)(2,1)S(1)}, bf16[896,256]{1,0:T(8,128)(2,1)S(1)}, u32[]{:S(2)}, u32[]{:S(2)}) collective-permute-start(bf16[896,256]{1,0:T(8,128)(2,1)S(1)} %collective-permute-done.2), channel_id=1, source_target_pairs={{0,2},{2,4},{4,6},{6,8},{8,10},{10,12},{12,14},{14,16},{16,18},{18... | collective-permute-start | bytes 1376264 | tf_op jit(solution)/shard_map/ppermute | solution.py:17
  58.1 26.2 %collective-permute-start.10 = (bf16[896,256]{1,0:T(8,128)(2,1)S(1)}, bf16[896,256]{1,0:T(8,128)(2,1)S(1)}, u32[]{:S(2)}, u32[]{:S(2)}) collective-permute-start(bf16[896,256]{1,0:T(8,128)(2,1)S(1)} %collective-permute-done.9), channel_id=1, source_target_pairs={{0,30},{2,0},{4,2},{6,4},{8,6},{10,8},{12,10},{14,12},{16,14},{18,... | collective-permute-start | bytes 1376264 | tf_op jit(solution)/shard_map/ppermute | solution.py:19
  84.3 26.4 %copy-start.10 = (bf16[896,256]{1,0:T(8,128)(2,1)}, bf16[896,256]{1,0:T(8,128)(2,1)S(1)}, u32[]{:S(2)}) copy-start(bf16[896,256]{1,0:T(8,128)(2,1)S(1)} %collective-permute-done.3) | copy-start | bytes 1376260
  84.3 26.4 %collective-permute-start.4 = (bf16[896,256]{1,0:T(8,128)(2,1)S(1)}, bf16[896,256]{1,0:T(8,128)(2,1)S(1)}, u32[]{:S(2)}, u32[]{:S(2)}) collective-permute-start(bf16[896,256]{1,0:T(8,128)(2,1)S(1)} %collective-permute-done.3), channel_id=1, source_target_pairs={{0,2},{2,4},{4,6},{6,8},{8,10},{10,12},{12,14},{14,16},{16,18},{18... | collective-permute-start | bytes 1376264 | tf_op jit(solution)/shard_map/ppermute | solution.py:17
  84.3 26.4 %collective-permute-start.11 = (bf16[896,256]{1,0:T(8,128)(2,1)S(1)}, bf16[896,256]{1,0:T(8,128)(2,1)}, u32[]{:S(2)}, u32[]{:S(2)}) collective-permute-start(bf16[896,256]{1,0:T(8,128)(2,1)S(1)} %collective-permute-done.10), channel_id=1, source_target_pairs={{0,30},{2,0},{4,2},{6,4},{8,6},{10,8},{12,10},{14,12},{16,14},{18,... | collective-permute-start | bytes 1376264 | tf_op jit(solution)/shard_map/ppermute | solution.py:19
  110.7 16.2 %collective-permute-start.5 = (bf16[896,256]{1,0:T(8,128)(2,1)S(1)}, bf16[896,256]{1,0:T(8,128)(2,1)}, u32[]{:S(2)}, u32[]{:S(2)}) collective-permute-start(bf16[896,256]{1,0:T(8,128)(2,1)S(1)} %collective-permute-done.4), channel_id=1, source_target_pairs={{0,2},{2,4},{4,6},{6,8},{8,10},{10,12},{12,14},{14,16},{16,18},{18... | collective-permute-start | bytes 1376264 | tf_op jit(solution)/shard_map/ppermute | solution.py:17
  110.7 16.2 %collective-permute-start.12 = (bf16[896,256]{1,0:T(8,128)(2,1)}, bf16[896,256]{1,0:T(8,128)(2,1)}, u32[]{:S(2)}, u32[]{:S(2)}) collective-permute-start(bf16[896,256]{1,0:T(8,128)(2,1)} %collective-permute-done.11), channel_id=1, source_target_pairs={{0,30},{2,0},{4,2},{6,4},{8,6},{10,8},{12,10},{14,12},{16,14},{18,... | collective-permute-start | bytes 1376264 | tf_op jit(solution)/shard_map/ppermute | solution.py:19
  126.9 22.2 %collective-permute-start.6 = (bf16[896,256]{1,0:T(8,128)(2,1)}, bf16[896,256]{1,0:T(8,128)(2,1)}, u32[]{:S(2)}, u32[]{:S(2)}) collective-permute-start(bf16[896,256]{1,0:T(8,128)(2,1)} %collective-permute-done.5), channel_id=1, source_target_pairs={{0,2},{2,4},{4,6},{6,8},{8,10},{10,12},{12,14},{14,16},{16,18},{18... | collective-permute-start | bytes 1376264 | tf_op jit(solution)/shard_map/ppermute | solution.py:17
  126.9 63.6 %copy-start.13 = (bf16[896,256]{1,0:T(8,128)(2,1)S(1)}, bf16[896,256]{1,0:T(8,128)(2,1)}, u32[]{:S(2)}) copy-start(bf16[896,256]{1,0:T(8,128)(2,1)} %copy-done.12) | copy-start | bytes 1376260
  126.9 64.4 %copy-start.11 = (bf16[896,256]{1,0:T(8,128)(2,1)S(1)}, bf16[896,256]{1,0:T(8,128)(2,1)}, u32[]{:S(2)}) copy-start(bf16[896,256]{1,0:T(8,128)(2,1)} %copy-done.10) | copy-start | bytes 1376260
  126.9 65.3 %copy-start.7 = (bf16[896,256]{1,0:T(8,128)(2,1)S(1)}, bf16[896,256]{1,0:T(8,128)(2,1)}, u32[]{:S(2)}) copy-start(bf16[896,256]{1,0:T(8,128)(2,1)} %copy-done.6) | copy-start | bytes 1376260
  126.9 66.1 %copy-start.3 = (bf16[896,256]{1,0:T(8,128)(2,1)S(1)}, bf16[896,256]{1,0:T(8,128)(2,1)}, u32[]{:S(2)}) copy-start(bf16[896,256]{1,0:T(8,128)(2,1)} %copy-done.2) | copy-start | bytes 1376260
  126.9 69.3 %copy-start.5 = (bf16[896,256]{1,0:T(8,128)(2,1)S(1)}, bf16[896,256]{1,0:T(8,128)(2,1)}, u32[]{:S(2)}) copy-start(bf16[896,256]{1,0:T(8,128)(2,1)} %copy-done.4) | copy-start | bytes 1376260
  126.9 70.2 %copy-start.9 = (bf16[896,256]{1,0:T(8,128)(2,1)S(1)}, bf16[896,256]{1,0:T(8,128)(2,1)}, u32[]{:S(2)}) copy-start(bf16[896,256]{1,0:T(8,128)(2,1)} %copy-done.8) | copy-start | bytes 1376260
  126.9 25.3 %collective-permute-start.13 = (bf16[896,256]{1,0:T(8,128)(2,1)}, bf16[896,256]{1,0:T(8,128)(2,1)S(1)}, u32[]{:S(2)}, u32[]{:S(2)}) collective-permute-start(bf16[896,256]{1,0:T(8,128)(2,1)} %collective-permute-done.12), channel_id=1, source_target_pairs={{0,30},{2,0},{4,2},{6,4},{8,6},{10,8},{12,10},{14,12},{16,14},{18,... | collective-permute-start | bytes 1376264 | tf_op jit(solution)/shard_map/ppermute | solution.py:19
  149.1 12.0 %collective-permute-start.7 = (bf16[896,256]{1,0:T(8,128)(2,1)}, bf16[896,256]{1,0:T(8,128)(2,1)S(1)}, u32[]{:S(2)}, u32[]{:S(2)}) collective-permute-start(bf16[896,256]{1,0:T(8,128)(2,1)} %collective-permute-done.6), channel_id=1, source_target_pairs={{0,2},{2,4},{4,6},{6,8},{8,10},{10,12},{12,14},{14,16},{16,18},{18... | collective-permute-start | bytes 1376264 | tf_op jit(solution)/shard_map/ppermute | solution.py:17
  152.2 51.0 %copy-start.14 = (f32[4096]{0:T(1024)S(1)}, f32[4096]{0:T(1024)}, u32[]{:S(2)}) copy-start(f32[4096]{0:T(1024)} %param.10) | copy-start | bytes 49156
  152.2 32.9 %collective-permute-start.14 = (bf16[896,256]{1,0:T(8,128)(2,1)S(1)}, bf16[896,256]{1,0:T(8,128)(2,1)S(1)}, u32[]{:S(2)}, u32[]{:S(2)}) collective-permute-start(bf16[896,256]{1,0:T(8,128)(2,1)S(1)} %collective-permute-done.13), channel_id=1, source_target_pairs={{0,30},{2,0},{4,2},{6,4},{8,6},{10,8},{12,10},{14,12},{16,14},{18,... | collective-permute-start | bytes 1376264 | tf_op jit(solution)/shard_map/ppermute | solution.py:19
  250.6 112.3 %copy-start.15 = (s32[256]{0:T(256)S(1)}, s32[256]{0:T(256)}, u32[]{:S(2)}) copy-start(s32[256]{0:T(256)} %param.17) | copy-start | bytes 3076
  250.6 109.2 %all-reduce.2.cloned.1.call-start = ((), (), s32[]{:S(2)}) async-start(), calls=%async_computation.4 | async-start | bytes 1048576 | tf_op jit(solution)/shard_map/psum | solution.py:68
  288.8 129.6 %all-gather.8.cloned.1.call-start = ((), (), s32[]{:S(2)}) async-start(), calls=%async_computation.5 | async-start | bytes 4456448 | tf_op jit(solution)/shard_map/all_gather | solution.py:70
  (4 other events, 30.3 us)
Sparse Core Ops, SparseCore 0:
  9.8 99.3 all-gather.3
  111.7 81.6 all-gather.5
  250.8 35.5 reduce-scatter.1
  289.0 70.8 all-reduce.1
  363.0 55.4 all-gather.7
